TPU v7x, 256 devices: a whole 4x4x8 slice. The times are simulated.
256 devices in a mesh: gx: 32 (over y, z), gy: 8 (over x, core).
Axes of the slice: x: 4, y: 4, z: 8, core: 2. Of those that a mesh axis runs over, the one named last changes fastest.
Arguments:
- densities: bfloat16 [24576, 32, 128], P(('gx', 'gy')), may hold values from -6 to 6
- geometry: float32 [24576, 7, 128], P(('gx', 'gy')), as said below
- near_ids: int32 [24576, 8], P(('gx', 'gy')), may hold values from 0 to 24575, as said below
- basis_in: bfloat16 [24576, 64, 128], P(('gx', 'gy')), may hold values from -0.5 to 0.5
- basis_out: bfloat16 [24576, 64, 128], P(('gx', 'gy')), may hold values from -0.75 to 0.75
- leaf_up: bfloat16 [24576, 64, 64], P(('gx', 'gy')), may hold values from -0.078125 to 0.078125
- leaf_down: bfloat16 [24576, 64, 64], P(('gx', 'gy')), may hold values from -0.75 to 0.75
- leaf_coupling: bfloat16 [24576, 6, 64, 64], P(('gx', 'gy')), may hold values from -0.3125 to 0.3125
- leaf_far: int32 [24576, 6], P(('gx', 'gy')), may hold values from 0 to 24575, as said below
- leaf_count: int32 [24576], P(('gx', 'gy')), may hold values from 1 to 6, as said below
- cluster_up: bfloat16 [256, 64, 64], P(('gx', 'gy')), may hold values from -0.25 to 0.25
- cluster_down: bfloat16 [256, 64, 64], P(('gx', 'gy')), may hold values from -0.75 to 0.75
- cluster_coupling: bfloat16 [256, 6, 64, 64], P(('gx', 'gy')), may hold values from -0.3125 to 0.3125
- cluster_far: int32 [256, 6], P(('gx', 'gy')), may hold values from 0 to 255, as said below
- group_up: bfloat16 [32, 64, 64], replicated, may hold values from -0.375 to 0.375
- group_down: bfloat16 [32, 64, 64], P('gx'), may hold values from -0.75 to 0.75
- group_coupling: bfloat16 [32, 6, 64, 64], P('gx'), may hold values from -0.3125 to 0.3125
- group_far: int32 [32, 6], P('gx'), may hold values from 0 to 31, as said below
- root_coupling: bfloat16 [8, 8, 64, 64], replicated, may hold values from -0.25 to 0.25
Outputs:
- potential: float32 [24576, 32, 128], P(('gx', 'gy'))
Inputs may be any that keep to these rules, and one draw needn't show every extreme that they name: `near_ids`: row l names 8 different leaves of a window of 9 consecutive leaves that contains l, centred on l where the ends allow. `leaf_far`: row l names 6 different leaves held by l's device or its two neighbours in leaf order, none within 4 leaves of l; only the first leaf_count[l] entries are used. `leaf_count`: every device holds a leaf with 6. `cluster_far`: row u names 6 different level-two clusters other than u, of u's group or the two groups beside it. `group_far`: row g names 6 different level-one clusters other than g. `geometry`: rows 0 to 2 hold a panel's centre, rows 3 to 5 its unit normal, row 6 its area, from 0.25 to 2.
All inputs are finite; a program needn't handle non-finite values.
Results may differ from a plain program's by a relative error of at most 0.012.
Values may be sent and summed in bfloat16 or wider, within the bound.
A program may use at most 128 MiB of HBM per device.

v0:
```python
import math
import jax
import jax.numpy as jnp
from jax import lax
from jax.sharding import PartitionSpec as P

REACH = 4
BRANCH = 4
four_pi = 4.0 * math.pi
leaf_block = 8


def padded(cells, sides, width):
    for axis, dim in sides:
        count = lax.axis_size(axis)
        ends = count - 1
        head = lax.slice_in_dim(cells, 0, width, axis=dim)
        tail = lax.slice_in_dim(cells, cells.shape[dim] - width, cells.shape[dim], axis=dim)
        cells = jnp.concatenate(
            [
                lax.ppermute(tail, axis, [(i, (i + 1) % count) for i in range(ends)]),
                cells,
                lax.ppermute(head, axis, [((i + 1) % count, i) for i in range(ends)]),
            ],
            axis=dim,
        )
    return cells


def near_kernel(target, source):
    offsets = [
        target[:, coord_id, :, None, None] - source[:, None, :, coord_id, :]
        for coord_id in range(3)
    ]
    distance = offsets[0] * offsets[0] + offsets[1] * offsets[1] + offsets[2] * offsets[2]
    facing = (
        source[:, None, :, 3, :] * offsets[0]
        + source[:, None, :, 4, :] * offsets[1]
        + source[:, None, :, 5, :] * offsets[2]
    )
    panel_area = source[:, None, :, 6, :]
    spread = distance + panel_area
    return panel_area * facing / (four_pi * spread * jnp.sqrt(spread))


def on_device(
    densities,
    geometry,
    near_ids,
    basis_in,
    basis_out,
    leaf_up,
    leaf_down,
    leaf_coupling,
    leaf_far,
    leaf_count,
    cluster_up,
    cluster_down,
    cluster_coupling,
    cluster_far,
    group_up,
    group_down,
    group_coupling,
    group_far,
    root_coupling,
):
    wide = jnp.float32
    narrow = jnp.bfloat16
    leaves = densities.shape[0]
    coeff_order = basis_in.shape[1]
    columns = densities.shape[1]
    flat = coeff_order * columns
    first_leaf = lax.axis_index(("gx", "gy")) * leaves
    gx_index = lax.axis_index("gx")
    group_size = lax.axis_size("gy")
    groups = lax.axis_size("gx")
    leaf_coeffs = jnp.einsum(
        "lkm,lrm->lkr", basis_in, densities, preferred_element_type=wide
    ).astype(narrow)
    mid_coeffs = jnp.einsum(
        "lik,lkr->ir", leaf_up, leaf_coeffs, preferred_element_type=wide
    ).astype(narrow)
    mid_term = jnp.dot(cluster_up[0], mid_coeffs, preferred_element_type=wide).reshape(1, flat)
    mid_flat = mid_coeffs.reshape(1, flat)
    siblings = lax.all_gather(mid_flat, "gy", axis=0, tiled=True)
    group_sum = lax.psum(mid_term, "gy")
    nearby = padded(siblings, (("gx", 0),), group_size)
    mid_picked = jnp.take(nearby, cluster_far[0] - (gx_index - 1) * group_size, axis=0)
    top_coeffs = lax.all_gather(group_sum.astype(narrow), "gx", axis=0, tiled=True)
    top_block = top_coeffs.reshape(groups, coeff_order, columns)
    root_terms = jnp.einsum("gik,gkr->gir", group_up, top_block, preferred_element_type=wide)
    root_coeffs = jnp.sum(
        root_terms.reshape(groups // BRANCH, BRANCH, coeff_order, columns), axis=1
    ).astype(narrow)
    root_row = lax.dynamic_index_in_dim(root_coupling, gx_index // BRANCH, 0, keepdims=False)
    root_field = jnp.einsum(
        "sik,skr->ir", root_row, root_coeffs, preferred_element_type=wide
    ).astype(narrow)
    top_picked = jnp.take(top_block, group_far[0], axis=0)
    top_field = (
        jnp.einsum("fik,fkr->ir", group_coupling[0], top_picked, preferred_element_type=wide)
        + jnp.dot(group_down[0], root_field, preferred_element_type=wide)
    ).astype(narrow)
    mid_block = mid_picked.reshape(-1, coeff_order, columns)
    mid_field = (
        jnp.einsum("fik,fkr->ir", cluster_coupling[0], mid_block, preferred_element_type=wide)
        + jnp.dot(cluster_down[0], top_field, preferred_element_type=wide)
    ).astype(narrow)
    coeff_rim = padded(leaf_coeffs.reshape(leaves, flat), ((("gx", "gy"), 0),), leaves)
    picked = jnp.take(coeff_rim, leaf_far - (first_leaf - leaves), axis=0).reshape(
        leaves, -1, coeff_order, columns
    )
    live_mask = (lax.broadcasted_iota(jnp.int32, leaf_far.shape, 1) < leaf_count[:, None]).astype(
        narrow
    )
    picked = picked * live_mask[:, :, None, None]
    leaf_field = (
        jnp.einsum("lfik,lfkr->lir", leaf_coupling, picked, preferred_element_type=wide)
        + jnp.einsum("lik,kr->lir", leaf_down, mid_field, preferred_element_type=wide)
    ).astype(narrow)
    far_part = jnp.einsum("lkr,lkm->lrm", leaf_field, basis_out, preferred_element_type=wide)
    values_rim = padded(densities, ((("gx", "gy"), 0),), REACH)
    shape_rim = padded(geometry, ((("gx", "gy"), 0),), REACH)
    near_local = near_ids - (first_leaf - REACH)

    def near_block(pieces):
        target, indices = pieces
        source = jnp.take(shape_rim, indices, axis=0)
        values = jnp.take(values_rim, indices, axis=0)
        kernel = near_kernel(target, source).astype(narrow)
        return jnp.einsum("bmnj,bnrj->brm", kernel, values, preferred_element_type=wide)

    near_part = lax.map(
        near_block,
        (
            geometry.reshape(leaves // leaf_block, leaf_block, 7, -1),
            near_local.reshape(leaves // leaf_block, leaf_block, -1),
        ),
    )
    return far_part + near_part.reshape(far_part.shape)


def solution(mesh):
    return jax.shard_map(
        on_device,
        mesh=mesh,
        in_specs=(
            P(("gx", "gy"), None, None),
            P(("gx", "gy"), None, None),
            P(("gx", "gy"), None),
            P(("gx", "gy"), None, None),
            P(("gx", "gy"), None, None),
            P(("gx", "gy"), None, None),
            P(("gx", "gy"), None, None),
            P(("gx", "gy"), None, None, None),
            P(("gx", "gy"), None),
            P(("gx", "gy")),
            P(("gx", "gy"), None, None),
            P(("gx", "gy"), None, None),
            P(("gx", "gy"), None, None, None),
            P(("gx", "gy"), None),
            P(),
            P("gx", None, None),
            P("gx", None, None, None),
            P("gx", None),
            P(),
        ),
        out_specs=P(("gx", "gy"), None, None),
        check_vma=False,
    )
```

profile of v0, /device:TPU:8, one launch (start us, length us, event | category | flops | bytes accessed | tf_op | source)
XLA Modules:
  0.0 328.0 jit_solution(2928487035204301218)
XLA Ops:
  0.0 2.6 convolution_convert_fusion
  2.6 1.3 copy.65
  4.0 1.0 copy.66
  4.9 9.3 %collective-permute-start.1 = (bf16[96,2048]{1,0:T(8,128)(2,1)}, bf16[96,2048]{1,0:T(8,128)(2,1)}, u32[]{:S(2)}, u32[]{:S(2)}) collective-permute-start(bf16[96,2048]{1,0:T(8,128)(2,1)} %copy.66), channel_id=1, source_target_pairs={{1,0},{2,1},{3,2},{4,3},{5,4},{6,5},{7,6},{8,7},{9,8},{10,9},{11,1... | collective-permute-start | bytes 1179656 | tf_op jit(solution)/shard_map/ppermute | solution.py:23
  14.2 1.9 collective-permute-start
  16.2 1.2 copy.80
  17.4 1.9 collective-permute-start.6
  19.3 8.0 %collective-permute-start.7 = (f32[4,7,128]{2,1,0:T(8,128)S(1)}, f32[4,7,128]{2,1,0:T(8,128)S(1)}, u32[]{:S(2)}, u32[]{:S(2)}) collective-permute-start(f32[4,7,128]{2,1,0:T(8,128)S(1)} %get-tuple-element.83), channel_id=1, source_target_pairs={{1,0},{2,1},{3,2},{4,3},{5,4},{6,5},{7,6},{8,7},{9,8},{10,9},{11,1... | collective-permute-start | bytes 43016 | tf_op jit(solution)/shard_map/ppermute | solution.py:23
  27.3 4.0 %copy.72 = bf16[96,64,64]{2,1,0:T(8,128)(2,1)} copy(bf16[96,64,64]{0,2,1:T(8,128)(2,1)} %param.26) | data formatting | bytes 1572864 | tf_op args[5]
  31.4 2.0 fusion.35
  33.5 12.8 %all-gather = bf16[8,1,2048]{2,1,0:T(2,128)(2,1)S(1)} all-gather(bf16[1,1,2048]{2,1,0:T(2,128)(2,1)S(1)} %reshape.240), channel_id=1, replica_groups=mesh['gx'=32,'gy'=8] {'gy'}, dimensions={0}, use_global_device_ids=true | all-gather | bytes 36864 | tf_op jit(solution)/shard_map/all_gather | solution.py:85
  46.3 1.9 collective-permute-start.3
  48.4 0.8 fusion.62
  50.4 24.5 %psum.7 = bf16[1,2048]{1,0:T(2,128)(2,1)S(1)} all-reduce(f32[1,2048]{1,0:T(1,128)S(1)} %reshape.189), channel_id=1, replica_groups=mesh['gx'=32,'gy'=8] {'gy'}, use_global_device_ids=true, to_apply=%region_0.0 | all-reduce | flops 2048 | bytes 12288 | tf_op jit(solution)/shard_map/psum | solution.py:86
  74.9 48.0 %all-gather.1 = bf16[32,1,2048]{2,1,0:T(2,128)(2,1)S(1)} all-gather(bf16[1,1,2048]{2,1,0:T(2,128)(2,1)S(1)} %bitcast.169), channel_id=1, replica_groups=mesh['gx'=32,'gy'=8] {'gx'}, dimensions={0}, use_global_device_ids=true | all-gather | bytes 135168 | tf_op jit(solution)/shard_map/all_gather | solution.py:89
  125.1 1.1 convolution_bitcast_fusion.1
  126.2 1.8 fusion.33
  129.4 4.0 %copy.78 = bf16[96,64,64]{2,1,0:T(8,128)(2,1)} copy(bf16[96,64,64]{0,2,1:T(8,128)(2,1)} %param.27) | data formatting | bytes 1572864 | tf_op args[6]
  133.4 16.1 %copy.71 = bf16[96,6,64,64]{3,2,1,0:T(8,128)(2,1)} copy(bf16[96,6,64,64]{0,3,2,1:T(8,128)(2,1)} %param.28) | data formatting | bytes 9437184 | tf_op args[7]
  149.5 2.4 collective-permute-start.2
  152.0 1.9 collective-permute-start.4
  154.0 8.0 %collective-permute-start.5 = (bf16[4,32,128]{2,1,0:T(8,128)(2,1)S(1)}, bf16[4,32,128]{2,1,0:T(8,128)(2,1)S(1)}, u32[]{:S(2)}, u32[]{:S(2)}) collective-permute-start(bf16[4,32,128]{2,1,0:T(8,128)(2,1)S(1)} %get-tuple-element.81), channel_id=1, source_target_pairs={{1,0},{2,1},{3,2},{4,3},{5,4},{6,5},{7,6},{8,7},{9,8},{10,9},{11,1... | collective-permute-start | bytes 98312 | tf_op jit(solution)/shard_map/ppermute | solution.py:23
  163.5 1.2 pad_maximum_fusion.1
  164.7 130.7 %while.10 = (s32[]{:T(128)}, f32[12,8,32,128]{3,2,1,0:T(8,128)}, s32[12,8,8]{2,1,0:T(8,128)}, bf16[104,32,128]{2,1,0:T(8,128)(2,1)S(1)}, f32[104,7,128]{2,1,0:T(...) while((s32[]{:T(128)}, f32[12,8,32,128]{3,2,1,0:T(8,128)}, s32[12,8,8]{2,1,0:T(8,128)}, ...), condition=%wide.region_3.4_spmd, body=%wide.region_2.3_spmd.sunk | while | flops 87352896 | bytes 3410213 | solution.py:133
  166.2 0.8 dynamic-slice_bitcast_fusion.2
  168.3 0.8 fusion.83
  169.7 5.9 %fusion.84 = f32[12,8,32,128]{3,2,1,0:T(8,128)} fusion(f32[12,8,32,128]{3,2,1,0:T(8,128)} %get-tuple-element.149, s32[]{:T(128)S(6)} %copy.97, f32[8,8,128]{2,1,0:T(8,128)S(1)} %bitcast.159, f32[8,128]{1,0:T(8,128)} %get-tuple-element.132, f32[8,8,128]{2,1,0:T(8,128)S(1)} %bitcast.160, f32[8,8,128]{2,1,0:T(8,128)S(1)} %bitcast.161, ...), kind=kOutput, calls=%fused_computation.21.clone.1 | convolution fusion | flops 87293952 | bytes 897092 | tf_op jit(solution)/shard_map/while/body/eval_jaxpr/bmnj,bnrj->brm/dot_general | solution.py:131
  177.1 0.8 dynamic-slice_bitcast_fusion.2
  179.2 0.8 fusion.83
  180.6 5.9 %fusion.84 = f32[12,8,32,128]{3,2,1,0:T(8,128)} fusion(f32[12,8,32,128]{3,2,1,0:T(8,128)} %get-tuple-element.149, s32[]{:T(128)S(6)} %copy.97, f32[8,8,128]{2,1,0:T(8,128)S(1)} %bitcast.159, f32[8,128]{1,0:T(8,128)} %get-tuple-element.132, f32[8,8,128]{2,1,0:T(8,128)S(1)} %bitcast.160, f32[8,8,128]{2,1,0:T(8,128)S(1)} %bitcast.161, ...), kind=kOutput, calls=%fused_computation.21.clone.1 | convolution fusion | flops 87293952 | bytes 897092 | tf_op jit(solution)/shard_map/while/body/eval_jaxpr/bmnj,bnrj->brm/dot_general | solution.py:131
  188.0 0.8 dynamic-slice_bitcast_fusion.2
  190.1 0.8 fusion.83
  191.5 5.9 %fusion.84 = f32[12,8,32,128]{3,2,1,0:T(8,128)} fusion(f32[12,8,32,128]{3,2,1,0:T(8,128)} %get-tuple-element.149, s32[]{:T(128)S(6)} %copy.97, f32[8,8,128]{2,1,0:T(8,128)S(1)} %bitcast.159, f32[8,128]{1,0:T(8,128)} %get-tuple-element.132, f32[8,8,128]{2,1,0:T(8,128)S(1)} %bitcast.160, f32[8,8,128]{2,1,0:T(8,128)S(1)} %bitcast.161, ...), kind=kOutput, calls=%fused_computation.21.clone.1 | convolution fusion | flops 87293952 | bytes 897092 | tf_op jit(solution)/shard_map/while/body/eval_jaxpr/bmnj,bnrj->brm/dot_general | solution.py:131
  198.9 0.8 dynamic-slice_bitcast_fusion.2
  201.0 0.8 fusion.83
  202.4 5.9 %fusion.84 = f32[12,8,32,128]{3,2,1,0:T(8,128)} fusion(f32[12,8,32,128]{3,2,1,0:T(8,128)} %get-tuple-element.149, s32[]{:T(128)S(6)} %copy.97, f32[8,8,128]{2,1,0:T(8,128)S(1)} %bitcast.159, f32[8,128]{1,0:T(8,128)} %get-tuple-element.132, f32[8,8,128]{2,1,0:T(8,128)S(1)} %bitcast.160, f32[8,8,128]{2,1,0:T(8,128)S(1)} %bitcast.161, ...), kind=kOutput, calls=%fused_computation.21.clone.1 | convolution fusion | flops 87293952 | bytes 897092 | tf_op jit(solution)/shard_map/while/body/eval_jaxpr/bmnj,bnrj->brm/dot_general | solution.py:131
  209.8 0.8 dynamic-slice_bitcast_fusion.2
  211.9 0.8 fusion.83
  213.3 5.9 %fusion.84 = f32[12,8,32,128]{3,2,1,0:T(8,128)} fusion(f32[12,8,32,128]{3,2,1,0:T(8,128)} %get-tuple-element.149, s32[]{:T(128)S(6)} %copy.97, f32[8,8,128]{2,1,0:T(8,128)S(1)} %bitcast.159, f32[8,128]{1,0:T(8,128)} %get-tuple-element.132, f32[8,8,128]{2,1,0:T(8,128)S(1)} %bitcast.160, f32[8,8,128]{2,1,0:T(8,128)S(1)} %bitcast.161, ...), kind=kOutput, calls=%fused_computation.21.clone.1 | convolution fusion | flops 87293952 | bytes 897092 | tf_op jit(solution)/shard_map/while/body/eval_jaxpr/bmnj,bnrj->brm/dot_general | solution.py:131
  220.6 0.8 dynamic-slice_bitcast_fusion.2
  222.8 0.8 fusion.83
  224.2 5.9 %fusion.84 = f32[12,8,32,128]{3,2,1,0:T(8,128)} fusion(f32[12,8,32,128]{3,2,1,0:T(8,128)} %get-tuple-element.149, s32[]{:T(128)S(6)} %copy.97, f32[8,8,128]{2,1,0:T(8,128)S(1)} %bitcast.159, f32[8,128]{1,0:T(8,128)} %get-tuple-element.132, f32[8,8,128]{2,1,0:T(8,128)S(1)} %bitcast.160, f32[8,8,128]{2,1,0:T(8,128)S(1)} %bitcast.161, ...), kind=kOutput, calls=%fused_computation.21.clone.1 | convolution fusion | flops 87293952 | bytes 897092 | tf_op jit(solution)/shard_map/while/body/eval_jaxpr/bmnj,bnrj->brm/dot_general | solution.py:131
  231.5 0.8 dynamic-slice_bitcast_fusion.2
  233.7 0.8 fusion.83
  235.1 5.9 %fusion.84 = f32[12,8,32,128]{3,2,1,0:T(8,128)} fusion(f32[12,8,32,128]{3,2,1,0:T(8,128)} %get-tuple-element.149, s32[]{:T(128)S(6)} %copy.97, f32[8,8,128]{2,1,0:T(8,128)S(1)} %bitcast.159, f32[8,128]{1,0:T(8,128)} %get-tuple-element.132, f32[8,8,128]{2,1,0:T(8,128)S(1)} %bitcast.160, f32[8,8,128]{2,1,0:T(8,128)S(1)} %bitcast.161, ...), kind=kOutput, calls=%fused_computation.21.clone.1 | convolution fusion | flops 87293952 | bytes 897092 | tf_op jit(solution)/shard_map/while/body/eval_jaxpr/bmnj,bnrj->brm/dot_general | solution.py:131
  242.4 0.8 dynamic-slice_bitcast_fusion.2
  244.6 0.8 fusion.83
  246.0 5.9 %fusion.84 = f32[12,8,32,128]{3,2,1,0:T(8,128)} fusion(f32[12,8,32,128]{3,2,1,0:T(8,128)} %get-tuple-element.149, s32[]{:T(128)S(6)} %copy.97, f32[8,8,128]{2,1,0:T(8,128)S(1)} %bitcast.159, f32[8,128]{1,0:T(8,128)} %get-tuple-element.132, f32[8,8,128]{2,1,0:T(8,128)S(1)} %bitcast.160, f32[8,8,128]{2,1,0:T(8,128)S(1)} %bitcast.161, ...), kind=kOutput, calls=%fused_computation.21.clone.1 | convolution fusion | flops 87293952 | bytes 897092 | tf_op jit(solution)/shard_map/while/body/eval_jaxpr/bmnj,bnrj->brm/dot_general | solution.py:131
  255.4 0.8 fusion.83
  256.9 5.9 %fusion.84 = f32[12,8,32,128]{3,2,1,0:T(8,128)} fusion(f32[12,8,32,128]{3,2,1,0:T(8,128)} %get-tuple-element.149, s32[]{:T(128)S(6)} %copy.97, f32[8,8,128]{2,1,0:T(8,128)S(1)} %bitcast.159, f32[8,128]{1,0:T(8,128)} %get-tuple-element.132, f32[8,8,128]{2,1,0:T(8,128)S(1)} %bitcast.160, f32[8,8,128]{2,1,0:T(8,128)S(1)} %bitcast.161, ...), kind=kOutput, calls=%fused_computation.21.clone.1 | convolution fusion | flops 87293952 | bytes 897092 | tf_op jit(solution)/shard_map/while/body/eval_jaxpr/bmnj,bnrj->brm/dot_general | solution.py:131
  264.2 0.8 dynamic-slice_bitcast_fusion.2
  266.3 0.8 fusion.83
  267.8 5.9 %fusion.84 = f32[12,8,32,128]{3,2,1,0:T(8,128)} fusion(f32[12,8,32,128]{3,2,1,0:T(8,128)} %get-tuple-element.149, s32[]{:T(128)S(6)} %copy.97, f32[8,8,128]{2,1,0:T(8,128)S(1)} %bitcast.159, f32[8,128]{1,0:T(8,128)} %get-tuple-element.132, f32[8,8,128]{2,1,0:T(8,128)S(1)} %bitcast.160, f32[8,8,128]{2,1,0:T(8,128)S(1)} %bitcast.161, ...), kind=kOutput, calls=%fused_computation.21.clone.1 | convolution fusion | flops 87293952 | bytes 897092 | tf_op jit(solution)/shard_map/while/body/eval_jaxpr/bmnj,bnrj->brm/dot_general | solution.py:131
  275.1 0.8 dynamic-slice_bitcast_fusion.2
  277.2 0.8 fusion.83
  278.7 5.9 %fusion.84 = f32[12,8,32,128]{3,2,1,0:T(8,128)} fusion(f32[12,8,32,128]{3,2,1,0:T(8,128)} %get-tuple-element.149, s32[]{:T(128)S(6)} %copy.97, f32[8,8,128]{2,1,0:T(8,128)S(1)} %bitcast.159, f32[8,128]{1,0:T(8,128)} %get-tuple-element.132, f32[8,8,128]{2,1,0:T(8,128)S(1)} %bitcast.160, f32[8,8,128]{2,1,0:T(8,128)S(1)} %bitcast.161, ...), kind=kOutput, calls=%fused_computation.21.clone.1 | convolution fusion | flops 87293952 | bytes 897092 | tf_op jit(solution)/shard_map/while/body/eval_jaxpr/bmnj,bnrj->brm/dot_general | solution.py:131
  288.1 0.8 fusion.83
  289.6 5.9 %fusion.84 = f32[12,8,32,128]{3,2,1,0:T(8,128)} fusion(f32[12,8,32,128]{3,2,1,0:T(8,128)} %get-tuple-element.149, s32[]{:T(128)S(6)} %copy.97, f32[8,8,128]{2,1,0:T(8,128)S(1)} %bitcast.159, f32[8,128]{1,0:T(8,128)} %get-tuple-element.132, f32[8,8,128]{2,1,0:T(8,128)S(1)} %bitcast.160, f32[8,8,128]{2,1,0:T(8,128)S(1)} %bitcast.161, ...), kind=kOutput, calls=%fused_computation.21.clone.1 | convolution fusion | flops 87293952 | bytes 897092 | tf_op jit(solution)/shard_map/while/body/eval_jaxpr/bmnj,bnrj->brm/dot_general | solution.py:131
  295.4 1.1 convolution_bitcast_fusion.3
  296.5 4.3 %fusion.37 = f32[32,96,64]{2,0,1:T(8,128)} fusion(bf16[96,64,64]{2,1,0:T(8,128)(2,1)} %copy.78, f32[32,64]{1,0:T(8,128)S(1)} %convolution_bitcast_fusion.3, bf16[32,64]{1,0:T(8,128)(2,1)} %fusion.33, bf16[1,64,64]{2,1,0:T(8,128)(2,1)} %param.32), kind=kOutput, calls=%fused_computation.60 | convolution fusion | flops 25432064 | bytes 1593344 | tf_op jit(solution)/shard_map/lik,kr->lir/dot_general | solution.py:119
  300.8 1.3 pad_maximum_fusion
  302.1 4.0 %gather_fusion.2 = bf16[576,2048]{1,0:T(8,128)(2,1)} fusion(bf16[288,2048]{1,0:T(8,128)(2,1)S(1)} %pad_maximum_fusion, s32[1024]{0:T(1024)S(1)} %pad_clamp_fusion.3), kind=kCustom, calls=%fused_computation.2 | custom fusion | bytes 4720896 | tf_op jit(solution)/shard_map/jit(_take)/gather | solution.py:110
  306.1 11.7 %gather.23 = bf16[96,6,64,32]{3,2,1,0:T(8,128)(2,1)} reshape(bf16[576,2048]{1,0:T(8,128)(2,1)} %gather_fusion.2) | data formatting | bytes 4718592 | tf_op jit(solution)/shard_map/jit(_take)/gather | solution.py:110
  317.8 10.3 %bitcast_add_fusion.1 = f32[96,32,128]{2,1,0:T(8,128)} fusion(f32[12,8,32,128]{3,2,1,0:T(8,128)} %get-tuple-element.37, bf16[96,64,128]{2,1,0:T(8,128)(2,1)S(1)} %copy-done, f32[32,96,64]{2,0,1:T(8,128)S(1)} %copy-done.1, bf16[96,6,64,64]{3,2,1,0:T(8,128)(2,1)} %copy.71, bf16[96,6,64,32]{3,2,1,0:T(8,128)(2,1)} %gather.23, pred[96,6]{1,0:T(8,128)(4,1)S(1)} %copy-done.6, ...), kind=kOutput, calls=%fused_computation.44 | convolution fusion | flops 204472320 | bytes 12584640 | tf_op jit(solution)/shard_map/lkr,lkm->lrm/dot_general | solution.py:121
  (161 shorter events, 49.6 us)
Async XLA Ops:
  0.0 317.8 %copy-start = (bf16[96,64,128]{2,1,0:T(8,128)(2,1)S(1)}, bf16[96,64,128]{2,1,0:T(8,128)(2,1)}, u32[]{:S(2)}) copy-start(bf16[96,64,128]{2,1,0:T(8,128)(2,1)} %param.25) | copy-start | bytes 4718596
  4.9 295.9 %collective-permute-start.1 = (bf16[96,2048]{1,0:T(8,128)(2,1)}, bf16[96,2048]{1,0:T(8,128)(2,1)}, u32[]{:S(2)}, u32[]{:S(2)}) collective-permute-start(bf16[96,2048]{1,0:T(8,128)(2,1)} %copy.66), channel_id=1, source_target_pairs={{1,0},{2,1},{3,2},{4,3},{5,4},{6,5},{7,6},{8,7},{9,8},{10,9},{11,1... | collective-permute-start | bytes 1179656 | tf_op jit(solution)/shard_map/ppermute | solution.py:23
  14.2 286.6 %collective-permute-start = (bf16[96,2048]{1,0:T(8,128)(2,1)}, bf16[96,2048]{1,0:T(8,128)(2,1)}, u32[]{:S(2)}, u32[]{:S(2)}) collective-permute-start(bf16[96,2048]{1,0:T(8,128)(2,1)} %copy.66), channel_id=1, source_target_pairs={{0,1},{1,2},{2,3},{3,4},{4,5},{5,6},{6,7},{7,8},{8,9},{9,10},{10,1... | collective-permute-start | bytes 1179656 | tf_op jit(solution)/shard_map/ppermute | solution.py:21
  17.4 132.2 %collective-permute-start.6 = (f32[4,7,128]{2,1,0:T(8,128)S(1)}, f32[4,7,128]{2,1,0:T(8,128)S(1)}, u32[]{:S(2)}, u32[]{:S(2)}) collective-permute-start(f32[4,7,128]{2,1,0:T(8,128)S(1)} %get-tuple-element.82), channel_id=1, source_target_pairs={{0,1},{1,2},{2,3},{3,4},{4,5},{5,6},{6,7},{7,8},{8,9},{9,10},{10,1... | collective-permute-start | bytes 43016 | tf_op jit(solution)/shard_map/ppermute | solution.py:21
  19.3 29.0 %copy-start.10 = (s32[1,6]{1,0:T(1,128)S(1)}, s32[1,6]{1,0:T(1,128)}, u32[]{:S(2)}) copy-start(s32[1,6]{1,0:T(1,128)} %param.34) | copy-start | bytes 76
  19.3 29.0 %copy-start.11 = (s32[1,6]{1,0:T(1,128)S(1)}, s32[1,6]{1,0:T(1,128)}, u32[]{:S(2)}) copy-start(s32[1,6]{1,0:T(1,128)} %param.38) | copy-start | bytes 76
  19.3 29.8 %copy-start.9 = (s32[96]{0:T(128)S(1)}, s32[96]{0:T(128)}, u32[]{:S(2)}) copy-start(s32[96]{0:T(128)} %param.30) | copy-start | bytes 1156
  19.3 30.5 %copy-start.7 = (s32[96,6]{0,1:T(8,128)S(1)}, s32[96,6]{0,1:T(8,128)}, u32[]{:S(2)}) copy-start(s32[96,6]{0,1:T(8,128)} %param.29) | copy-start | bytes 6916
  19.3 30.8 %copy-start.4 = (bf16[1,64,64]{2,1,0:T(8,128)(2,1)S(1)}, bf16[1,64,64]{2,1,0:T(8,128)(2,1)}, u32[]{:S(2)}) copy-start(bf16[1,64,64]{2,1,0:T(8,128)(2,1)} %param.31) | copy-start | bytes 24580
  19.3 132.6 %collective-permute-start.7 = (f32[4,7,128]{2,1,0:T(8,128)S(1)}, f32[4,7,128]{2,1,0:T(8,128)S(1)}, u32[]{:S(2)}, u32[]{:S(2)}) collective-permute-start(f32[4,7,128]{2,1,0:T(8,128)S(1)} %get-tuple-element.83), channel_id=1, source_target_pairs={{1,0},{2,1},{3,2},{4,3},{5,4},{6,5},{7,6},{8,7},{9,8},{10,9},{11,1... | collective-permute-start | bytes 43016 | tf_op jit(solution)/shard_map/ppermute | solution.py:23
  31.4 92.7 %copy-start.2 = (bf16[32,64,64]{2,1,0:T(8,128)(2,1)S(1)}, bf16[32,64,64]{2,1,0:T(8,128)(2,1)}, u32[]{:S(2)}) copy-start(bf16[32,64,64]{2,1,0:T(8,128)(2,1)} %param.35) | copy-start | bytes 786436
  31.4 93.7 %copy-start.8 = (s32[96,8]{0,1:T(8,128)S(1)}, s32[96,8]{0,1:T(8,128)}, u32[]{:S(2)}) copy-start(s32[96,8]{0,1:T(8,128)} %param.23) | copy-start | bytes 9220
  33.3 92.9 %copy-start.5 = (bf16[1,64,64]{2,1,0:T(8,128)(2,1)S(1)}, bf16[1,64,64]{2,1,0:T(8,128)(2,1)}, u32[]{:S(2)}) copy-start(bf16[1,64,64]{2,1,0:T(8,128)(2,1)} %param.36) | copy-start | bytes 24580
  46.3 107.6 %collective-permute-start.3 = (bf16[8,2048]{1,0:T(8,128)(2,1)S(1)}, bf16[8,2048]{1,0:T(8,128)(2,1)S(1)}, u32[]{:S(2)}, u32[]{:S(2)}) collective-permute-start(bf16[8,2048]{1,0:T(8,128)(2,1)S(1)} %bitcast.165), channel_id=1, source_target_pairs={{8,0},{16,8},{24,16},{32,24},{40,32},{48,40},{56,48},{64,56},{72,6... | collective-permute-start | bytes 98312 | tf_op jit(solution)/shard_map/ppermute | solution.py:23
  149.5 12.5 %collective-permute-start.2 = (bf16[8,2048]{1,0:T(8,128)(2,1)S(1)}, bf16[8,2048]{1,0:T(8,128)(2,1)S(1)}, u32[]{:S(2)}, u32[]{:S(2)}) collective-permute-start(bf16[8,2048]{1,0:T(8,128)(2,1)S(1)} %bitcast.166), channel_id=1, source_target_pairs={{0,8},{8,16},{16,24},{24,32},{32,40},{40,48},{48,56},{56,64},{64,7... | collective-permute-start | bytes 98312 | tf_op jit(solution)/shard_map/ppermute | solution.py:21
  152.0 11.5 %collective-permute-start.4 = (bf16[4,32,128]{2,1,0:T(8,128)(2,1)S(1)}, bf16[4,32,128]{2,1,0:T(8,128)(2,1)S(1)}, u32[]{:S(2)}, u32[]{:S(2)}) collective-permute-start(bf16[4,32,128]{2,1,0:T(8,128)(2,1)S(1)} %get-tuple-element.80), channel_id=1, source_target_pairs={{0,1},{1,2},{2,3},{3,4},{4,5},{5,6},{6,7},{7,8},{8,9},{9,10},{10,1... | collective-permute-start | bytes 98312 | tf_op jit(solution)/shard_map/ppermute | solution.py:21
  154.0 9.5 %collective-permute-start.5 = (bf16[4,32,128]{2,1,0:T(8,128)(2,1)S(1)}, bf16[4,32,128]{2,1,0:T(8,128)(2,1)S(1)}, u32[]{:S(2)}, u32[]{:S(2)}) collective-permute-start(bf16[4,32,128]{2,1,0:T(8,128)(2,1)S(1)} %get-tuple-element.81), channel_id=1, source_target_pairs={{1,0},{2,1},{3,2},{4,3},{5,4},{6,5},{7,6},{8,7},{9,8},{10,9},{11,1... | collective-permute-start | bytes 98312 | tf_op jit(solution)/shard_map/ppermute | solution.py:23
  306.1 11.7 %copy-start.1 = (f32[32,96,64]{2,0,1:T(8,128)S(1)}, f32[32,96,64]{2,0,1:T(8,128)}, u32[]{:S(2)}) copy-start(f32[32,96,64]{2,0,1:T(8,128)} %fusion.37) | copy-start | bytes 2359300
  306.1 11.7 %copy-start.3 = (bf16[96,6]{1,0:T(8,128)(2,1)S(1)}, bf16[96,6]{1,0:T(8,128)(2,1)}, u32[]{:S(2)}) copy-start(bf16[96,6]{1,0:T(8,128)(2,1)} %fusion.49) | copy-start | bytes 3460
  306.1 11.7 %copy-start.6 = (pred[96,6]{1,0:T(8,128)(4,1)S(1)}, pred[96,6]{1,0:T(8,128)(4,1)}, u32[]{:S(2)}) copy-start(pred[96,6]{1,0:T(8,128)(4,1)} %copy.64) | copy-start | bytes 1732
where the time goes:
time: 331 us; the launch traced here: 328 us
  matrix products  94.2 us (28%)
  local copies, waits for them, and re-layouts  90.2 us (27%)
  blocking collectives  85.2 us (26%)
  starting transfers between devices  35.4 us (11%)
  other arithmetic  22.2 us (7%)
    dot_general x12, matrix products, near_block(): jnp.einsum('bmnj,bnrj->brm', kernel, values, preferred_element_type=wide)  70.5 us
    all_gather x1, blocking collectives, on_device(): lax.all_gather(group_sum.astype(narrow), 'gx', axis=0, tiled=True)  48 us
    ppermute x4, starting transfers between devices, padded(): lax.ppermute(head, axis, [((i + 1) % count, i) for i in range(ends)])  27.2 us
    unnamed x30, local copies, waits for them, and re-layouts  25.5 us
    psum x1, blocking collectives, on_device(): group_sum = lax.psum(mid_term, 'gy')  24.5 us
    gather x2, local copies, waits for them, and re-layouts, on_device(): jnp.take(coeff_rim, leaf_far - (first_leaf - leaves), axis=0)  15.6 us
    all_gather x1, blocking collectives, on_device(): siblings = lax.all_gather(mid_flat, 'gy', axis=0, tiled=True)  12.8 us
    dot_general x1, matrix products, on_device(): jnp.einsum('lkr,lkm->lrm', leaf_field, basis_out, preferred_element_type=...  10.3 us
  transfers between devices with their start and end apart: 8, of which 0 were waited for; matrix products, arithmetic and copies ran while one was open for 53% of the time, Pallas kernels for 0%

commit v1 on v0

--- a/solution.py
+++ b/solution.py
@@ -83,7 +83,13 @@
     mid_term = jnp.dot(cluster_up[0], mid_coeffs, preferred_element_type=wide).reshape(1, flat)
     mid_flat = mid_coeffs.reshape(1, flat)
     siblings = lax.all_gather(mid_flat, "gy", axis=0, tiled=True)
-    group_sum = lax.psum(mid_term, "gy")
+    n_dev = lax.axis_size("gy")
+    group_sum, stride = (mid_term, 1)
+    while stride < n_dev:
+        group_sum = group_sum + lax.ppermute(
+            group_sum, "gy", [(i_2, i_2 ^ stride) for i_2 in range(n_dev)]
+        )
+        stride = 2 * stride
     nearby = padded(siblings, (("gx", 0),), group_size)
     mid_picked = jnp.take(nearby, cluster_far[0] - (gx_index - 1) * group_size, axis=0)
     top_coeffs = lax.all_gather(group_sum.astype(narrow), "gx", axis=0, tiled=True)

time: 331 us -> 312 us (0.943)
  blocking collectives: 85.2 us -> 61.2 us
  waiting for transfers between devices: 0.02 us -> 3.67 us
    psum x1 -> x0, blocking collectives: 24.5 us -> none  [on_device(): group_sum = lax.psum(mid_term, 'gy')]
    ppermute x4, starting transfers between devices: 27.2 us -> 21.4 us  [padded(): lax.ppermute(head, axis, [((i + 1) % count, i) for i in range(ends)])]
    ppermute x0 -> x3, waiting for transfers between devices: none -> 3.65 us  [on_device(): lax.ppermute(group_sum, 'gy', [(i_2, i_2 ^ stride) for i_2 in range(n_dev)])]
  transfers between devices with their start and end apart: 8 -> 11, of which waited for: 0 -> 1; matrix products, arithmetic and copies ran while one was open for 53% -> 57% of each run, Pallas kernels for 0% -> 0%
where the time goes in v1:
time: 312 us; the launch traced here: 306 us
  matrix products  94.2 us (30%)
  local copies, waits for them, and re-layouts  91 us (29%)
  blocking collectives  61.2 us (20%)
  starting transfers between devices  32.7 us (10%)
  other arithmetic  22.8 us (7%)
  waiting for transfers between devices  3.67 us (1%)
    dot_general x12, matrix products, near_block(): jnp.einsum('bmnj,bnrj->brm', kernel, values, preferred_element_type=wide)  70.5 us
    all_gather x1, blocking collectives, on_device(): lax.all_gather(group_sum.astype(narrow), 'gx', axis=0, tiled=True)  48.5 us
    unnamed x30, local copies, waits for them, and re-layouts  26.1 us
    ppermute x4, starting transfers between devices, padded(): lax.ppermute(head, axis, [((i + 1) % count, i) for i in range(ends)])  21.4 us
    gather x2, local copies, waits for them, and re-layouts, on_device(): jnp.take(coeff_rim, leaf_far - (first_leaf - leaves), axis=0)  15.7 us
    all_gather x1, blocking collectives, on_device(): siblings = lax.all_gather(mid_flat, 'gy', axis=0, tiled=True)  12.8 us
    dot_general x1, matrix products, on_device(): jnp.einsum('lkr,lkm->lrm', leaf_field, basis_out, preferred_element_type=...  10.3 us
    ppermute x4, starting transfers between devices, padded(): lax.ppermute(tail, axis, [(i, (i + 1) % count) for i in range(ends)])  9.52 us
  transfers between devices with their start and end apart: 11, of which 1 were waited for; matrix products, arithmetic and copies ran while one was open for 57% of the time, Pallas kernels for 0%

profile of v1, /device:TPU:8, one launch (start us, length us, event | category | flops | bytes accessed | tf_op | source)
XLA Modules:
  0.0 306.3 jit_solution(16798051930908409114)
XLA Ops:
  0.0 2.6 convolution_convert_fusion
  2.6 1.3 copy.65
  4.0 1.0 copy.66
  4.9 9.3 %collective-permute-start.1 = (bf16[96,2048]{1,0:T(8,128)(2,1)}, bf16[96,2048]{1,0:T(8,128)(2,1)}, u32[]{:S(2)}, u32[]{:S(2)}) collective-permute-start(bf16[96,2048]{1,0:T(8,128)(2,1)} %copy.66), channel_id=1, source_target_pairs={{1,0},{2,1},{3,2},{4,3},{5,4},{6,5},{7,6},{8,7},{9,8},{10,9},{11,1... | collective-permute-start | bytes 1179656 | tf_op jit(solution)/shard_map/ppermute | solution.py:23
  14.2 1.9 collective-permute-start
  16.2 1.2 copy.80
  17.4 1.9 collective-permute-start.9
  19.4 8.0 %collective-permute-start.10 = (f32[4,7,128]{2,1,0:T(8,128)S(1)}, f32[4,7,128]{2,1,0:T(8,128)S(1)}, u32[]{:S(2)}, u32[]{:S(2)}) collective-permute-start(f32[4,7,128]{2,1,0:T(8,128)S(1)} %get-tuple-element.83), channel_id=1, source_target_pairs={{1,0},{2,1},{3,2},{4,3},{5,4},{6,5},{7,6},{8,7},{9,8},{10,9},{11,1... | collective-permute-start | bytes 43016 | tf_op jit(solution)/shard_map/ppermute | solution.py:23
  27.4 4.0 %copy.72 = bf16[96,64,64]{2,1,0:T(8,128)(2,1)} copy(bf16[96,64,64]{0,2,1:T(8,128)(2,1)} %param.26) | data formatting | bytes 1572864 | tf_op args[5]
  31.4 1.9 fusion.35
  34.3 0.8 fusion.62
  37.9 12.8 %all-gather = bf16[8,1,2048]{2,1,0:T(2,128)(2,1)S(1)} all-gather(bf16[1,1,2048]{2,1,0:T(2,128)(2,1)S(1)} %reshape.240), channel_id=1, replica_groups=mesh['gx'=32,'gy'=8] {'gy'}, dimensions={0}, use_global_device_ids=true | all-gather | bytes 36864 | tf_op jit(solution)/shard_map/all_gather | solution.py:85
  50.7 4.0 %copy.78 = bf16[96,64,64]{2,1,0:T(8,128)(2,1)} copy(bf16[96,64,64]{0,2,1:T(8,128)(2,1)} %param.27) | data formatting | bytes 1572864 | tf_op args[6]
  54.7 16.2 %copy.71 = bf16[96,6,64,64]{3,2,1,0:T(8,128)(2,1)} copy(bf16[96,6,64,64]{0,3,2,1:T(8,128)(2,1)} %param.28) | data formatting | bytes 9437184 | tf_op args[7]
  70.8 2.1 collective-permute-start.3
  72.9 3.8 %collective-permute-start.2 = (bf16[8,2048]{1,0:T(8,128)(2,1)S(1)}, bf16[8,2048]{1,0:T(8,128)(2,1)S(1)}, u32[]{:S(2)}, u32[]{:S(2)}) collective-permute-start(bf16[8,2048]{1,0:T(8,128)(2,1)S(1)} %bitcast.165), channel_id=1, source_target_pairs={{0,8},{8,16},{16,24},{24,32},{32,40},{40,48},{48,56},{56,64},{64,7... | collective-permute-start | bytes 98312 | tf_op jit(solution)/shard_map/ppermute | solution.py:21
  76.7 1.5 collective-permute-start.6
  78.3 3.6 %collective-permute-done.6 = f32[1,2048]{1,0:T(1,128)S(1)} collective-permute-done((f32[1,2048]{1,0:T(1,128)S(1)}, f32[1,2048]{1,0:T(1,128)S(1)}, u32[]{:S(2)}, u32[]{:S(2)}) %collective-permute-start.6) | collective-permute-done | bytes 8224 | tf_op jit(solution)/shard_map/ppermute | solution.py:89
  81.9 1.9 collective-permute-start.7
  83.9 48.5 %all-gather.1 = bf16[32,1,2048]{2,1,0:T(2,128)(2,1)S(1)} all-gather(bf16[1,1,2048]{2,1,0:T(2,128)(2,1)S(1)} %convert_bitcast_fusion), channel_id=1, replica_groups=mesh['gx'=32,'gy'=8] {'gx'}, dimensions={0}, use_global_device_ids=true | all-gather | bytes 135168 | tf_op jit(solution)/shard_map/all_gather | solution.py:95
  134.5 1.2 convolution_bitcast_fusion.1
  135.7 1.8 fusion.33
  137.5 2.1 collective-permute-start.8
  141.6 1.2 pad_maximum_fusion.1
  142.9 130.8 %while.10 = (s32[]{:T(128)}, f32[12,8,32,128]{3,2,1,0:T(8,128)}, s32[12,8,8]{2,1,0:T(8,128)}, bf16[104,32,128]{2,1,0:T(8,128)(2,1)S(1)}, f32[104,7,128]{2,1,0:T(...) while((s32[]{:T(128)}, f32[12,8,32,128]{3,2,1,0:T(8,128)}, s32[12,8,8]{2,1,0:T(8,128)}, ...), condition=%wide.region_2.3_spmd, body=%wide.region_1.2_spmd.sunk | while | flops 87352896 | bytes 3410213 | solution.py:139
  144.3 0.8 dynamic-slice_bitcast_fusion.2
  146.5 0.8 fusion.83
  147.9 5.9 %fusion.84 = f32[12,8,32,128]{3,2,1,0:T(8,128)} fusion(f32[12,8,32,128]{3,2,1,0:T(8,128)} %get-tuple-element.149, s32[]{:T(128)S(6)} %copy.97, f32[8,8,128]{2,1,0:T(8,128)S(1)} %bitcast.158, f32[8,128]{1,0:T(8,128)} %get-tuple-element.132, f32[8,8,128]{2,1,0:T(8,128)S(1)} %bitcast.159, f32[8,8,128]{2,1,0:T(8,128)S(1)} %bitcast.160, ...), kind=kOutput, calls=%fused_computation.21.clone.1 | convolution fusion | flops 87293952 | bytes 897092 | tf_op jit(solution)/shard_map/while/body/eval_jaxpr/bmnj,bnrj->brm/dot_general | solution.py:137
  155.2 0.8 dynamic-slice_bitcast_fusion.2
  157.4 0.8 fusion.83
  158.8 5.9 %fusion.84 = f32[12,8,32,128]{3,2,1,0:T(8,128)} fusion(f32[12,8,32,128]{3,2,1,0:T(8,128)} %get-tuple-element.149, s32[]{:T(128)S(6)} %copy.97, f32[8,8,128]{2,1,0:T(8,128)S(1)} %bitcast.158, f32[8,128]{1,0:T(8,128)} %get-tuple-element.132, f32[8,8,128]{2,1,0:T(8,128)S(1)} %bitcast.159, f32[8,8,128]{2,1,0:T(8,128)S(1)} %bitcast.160, ...), kind=kOutput, calls=%fused_computation.21.clone.1 | convolution fusion | flops 87293952 | bytes 897092 | tf_op jit(solution)/shard_map/while/body/eval_jaxpr/bmnj,bnrj->brm/dot_general | solution.py:137
  168.3 0.8 fusion.83
  169.7 5.9 %fusion.84 = f32[12,8,32,128]{3,2,1,0:T(8,128)} fusion(f32[12,8,32,128]{3,2,1,0:T(8,128)} %get-tuple-element.149, s32[]{:T(128)S(6)} %copy.97, f32[8,8,128]{2,1,0:T(8,128)S(1)} %bitcast.158, f32[8,128]{1,0:T(8,128)} %get-tuple-element.132, f32[8,8,128]{2,1,0:T(8,128)S(1)} %bitcast.159, f32[8,8,128]{2,1,0:T(8,128)S(1)} %bitcast.160, ...), kind=kOutput, calls=%fused_computation.21.clone.1 | convolution fusion | flops 87293952 | bytes 897092 | tf_op jit(solution)/shard_map/while/body/eval_jaxpr/bmnj,bnrj->brm/dot_general | solution.py:137
  177.0 0.8 dynamic-slice_bitcast_fusion.2
  179.2 0.8 fusion.83
  180.6 5.9 %fusion.84 = f32[12,8,32,128]{3,2,1,0:T(8,128)} fusion(f32[12,8,32,128]{3,2,1,0:T(8,128)} %get-tuple-element.149, s32[]{:T(128)S(6)} %copy.97, f32[8,8,128]{2,1,0:T(8,128)S(1)} %bitcast.158, f32[8,128]{1,0:T(8,128)} %get-tuple-element.132, f32[8,8,128]{2,1,0:T(8,128)S(1)} %bitcast.159, f32[8,8,128]{2,1,0:T(8,128)S(1)} %bitcast.160, ...), kind=kOutput, calls=%fused_computation.21.clone.1 | convolution fusion | flops 87293952 | bytes 897092 | tf_op jit(solution)/shard_map/while/body/eval_jaxpr/bmnj,bnrj->brm/dot_general | solution.py:137
  187.9 0.8 dynamic-slice_bitcast_fusion.2
  190.0 0.8 fusion.83
  191.5 5.9 %fusion.84 = f32[12,8,32,128]{3,2,1,0:T(8,128)} fusion(f32[12,8,32,128]{3,2,1,0:T(8,128)} %get-tuple-element.149, s32[]{:T(128)S(6)} %copy.97, f32[8,8,128]{2,1,0:T(8,128)S(1)} %bitcast.158, f32[8,128]{1,0:T(8,128)} %get-tuple-element.132, f32[8,8,128]{2,1,0:T(8,128)S(1)} %bitcast.159, f32[8,8,128]{2,1,0:T(8,128)S(1)} %bitcast.160, ...), kind=kOutput, calls=%fused_computation.21.clone.1 | convolution fusion | flops 87293952 | bytes 897092 | tf_op jit(solution)/shard_map/while/body/eval_jaxpr/bmnj,bnrj->brm/dot_general | solution.py:137
  201.0 0.8 fusion.83
  202.4 5.9 %fusion.84 = f32[12,8,32,128]{3,2,1,0:T(8,128)} fusion(f32[12,8,32,128]{3,2,1,0:T(8,128)} %get-tuple-element.149, s32[]{:T(128)S(6)} %copy.97, f32[8,8,128]{2,1,0:T(8,128)S(1)} %bitcast.158, f32[8,128]{1,0:T(8,128)} %get-tuple-element.132, f32[8,8,128]{2,1,0:T(8,128)S(1)} %bitcast.159, f32[8,8,128]{2,1,0:T(8,128)S(1)} %bitcast.160, ...), kind=kOutput, calls=%fused_computation.21.clone.1 | convolution fusion | flops 87293952 | bytes 897092 | tf_op jit(solution)/shard_map/while/body/eval_jaxpr/bmnj,bnrj->brm/dot_general | solution.py:137
  209.7 0.8 dynamic-slice_bitcast_fusion.2
  211.9 0.8 fusion.83
  213.3 5.9 %fusion.84 = f32[12,8,32,128]{3,2,1,0:T(8,128)} fusion(f32[12,8,32,128]{3,2,1,0:T(8,128)} %get-tuple-element.149, s32[]{:T(128)S(6)} %copy.97, f32[8,8,128]{2,1,0:T(8,128)S(1)} %bitcast.158, f32[8,128]{1,0:T(8,128)} %get-tuple-element.132, f32[8,8,128]{2,1,0:T(8,128)S(1)} %bitcast.159, f32[8,8,128]{2,1,0:T(8,128)S(1)} %bitcast.160, ...), kind=kOutput, calls=%fused_computation.21.clone.1 | convolution fusion | flops 87293952 | bytes 897092 | tf_op jit(solution)/shard_map/while/body/eval_jaxpr/bmnj,bnrj->brm/dot_general | solution.py:137
  220.6 0.8 dynamic-slice_bitcast_fusion.2
  222.8 0.8 fusion.83
  224.2 5.9 %fusion.84 = f32[12,8,32,128]{3,2,1,0:T(8,128)} fusion(f32[12,8,32,128]{3,2,1,0:T(8,128)} %get-tuple-element.149, s32[]{:T(128)S(6)} %copy.97, f32[8,8,128]{2,1,0:T(8,128)S(1)} %bitcast.158, f32[8,128]{1,0:T(8,128)} %get-tuple-element.132, f32[8,8,128]{2,1,0:T(8,128)S(1)} %bitcast.159, f32[8,8,128]{2,1,0:T(8,128)S(1)} %bitcast.160, ...), kind=kOutput, calls=%fused_computation.21.clone.1 | convolution fusion | flops 87293952 | bytes 897092 | tf_op jit(solution)/shard_map/while/body/eval_jaxpr/bmnj,bnrj->brm/dot_general | solution.py:137
  231.5 0.8 dynamic-slice_bitcast_fusion.2
  233.7 0.8 fusion.83
  235.1 5.9 %fusion.84 = f32[12,8,32,128]{3,2,1,0:T(8,128)} fusion(f32[12,8,32,128]{3,2,1,0:T(8,128)} %get-tuple-element.149, s32[]{:T(128)S(6)} %copy.97, f32[8,8,128]{2,1,0:T(8,128)S(1)} %bitcast.158, f32[8,128]{1,0:T(8,128)} %get-tuple-element.132, f32[8,8,128]{2,1,0:T(8,128)S(1)} %bitcast.159, f32[8,8,128]{2,1,0:T(8,128)S(1)} %bitcast.160, ...), kind=kOutput, calls=%fused_computation.21.clone.1 | convolution fusion | flops 87293952 | bytes 897092 | tf_op jit(solution)/shard_map/while/body/eval_jaxpr/bmnj,bnrj->brm/dot_general | solution.py:137
  242.4 0.8 dynamic-slice_bitcast_fusion.2
  244.6 0.8 fusion.83
  246.0 5.9 %fusion.84 = f32[12,8,32,128]{3,2,1,0:T(8,128)} fusion(f32[12,8,32,128]{3,2,1,0:T(8,128)} %get-tuple-element.149, s32[]{:T(128)S(6)} %copy.97, f32[8,8,128]{2,1,0:T(8,128)S(1)} %bitcast.158, f32[8,128]{1,0:T(8,128)} %get-tuple-element.132, f32[8,8,128]{2,1,0:T(8,128)S(1)} %bitcast.159, f32[8,8,128]{2,1,0:T(8,128)S(1)} %bitcast.160, ...), kind=kOutput, calls=%fused_computation.21.clone.1 | convolution fusion | flops 87293952 | bytes 897092 | tf_op jit(solution)/shard_map/while/body/eval_jaxpr/bmnj,bnrj->brm/dot_general | solution.py:137
  253.3 0.8 dynamic-slice_bitcast_fusion.2
  255.5 0.8 fusion.83
  256.9 5.9 %fusion.84 = f32[12,8,32,128]{3,2,1,0:T(8,128)} fusion(f32[12,8,32,128]{3,2,1,0:T(8,128)} %get-tuple-element.149, s32[]{:T(128)S(6)} %copy.97, f32[8,8,128]{2,1,0:T(8,128)S(1)} %bitcast.158, f32[8,128]{1,0:T(8,128)} %get-tuple-element.132, f32[8,8,128]{2,1,0:T(8,128)S(1)} %bitcast.159, f32[8,8,128]{2,1,0:T(8,128)S(1)} %bitcast.160, ...), kind=kOutput, calls=%fused_computation.21.clone.1 | convolution fusion | flops 87293952 | bytes 897092 | tf_op jit(solution)/shard_map/while/body/eval_jaxpr/bmnj,bnrj->brm/dot_general | solution.py:137
  266.4 0.8 fusion.83
  267.8 5.9 %fusion.84 = f32[12,8,32,128]{3,2,1,0:T(8,128)} fusion(f32[12,8,32,128]{3,2,1,0:T(8,128)} %get-tuple-element.149, s32[]{:T(128)S(6)} %copy.97, f32[8,8,128]{2,1,0:T(8,128)S(1)} %bitcast.158, f32[8,128]{1,0:T(8,128)} %get-tuple-element.132, f32[8,8,128]{2,1,0:T(8,128)S(1)} %bitcast.159, f32[8,8,128]{2,1,0:T(8,128)S(1)} %bitcast.160, ...), kind=kOutput, calls=%fused_computation.21.clone.1 | convolution fusion | flops 87293952 | bytes 897092 | tf_op jit(solution)/shard_map/while/body/eval_jaxpr/bmnj,bnrj->brm/dot_general | solution.py:137
  273.7 1.1 convolution_bitcast_fusion.3
  274.8 4.2 %fusion.37 = f32[32,96,64]{2,0,1:T(8,128)} fusion(bf16[96,64,64]{2,1,0:T(8,128)(2,1)} %copy.78, f32[32,64]{1,0:T(8,128)S(1)} %convolution_bitcast_fusion.3, bf16[32,64]{1,0:T(8,128)(2,1)} %fusion.33, bf16[1,64,64]{2,1,0:T(8,128)(2,1)} %param.32), kind=kOutput, calls=%fused_computation.60 | convolution fusion | flops 25432064 | bytes 1593344 | tf_op jit(solution)/shard_map/lik,kr->lir/dot_general | solution.py:125
  279.1 1.3 pad_maximum_fusion
  280.4 4.0 %gather_fusion.2 = bf16[576,2048]{1,0:T(8,128)(2,1)} fusion(bf16[288,2048]{1,0:T(8,128)(2,1)S(1)} %pad_maximum_fusion, s32[1024]{0:T(1024)S(1)} %pad_clamp_fusion.3), kind=kCustom, calls=%fused_computation.2 | custom fusion | bytes 4720896 | tf_op jit(solution)/shard_map/jit(_take)/gather | solution.py:116
  284.4 11.7 %gather.23 = bf16[96,6,64,32]{3,2,1,0:T(8,128)(2,1)} reshape(bf16[576,2048]{1,0:T(8,128)(2,1)} %gather_fusion.2) | data formatting | bytes 4718592 | tf_op jit(solution)/shard_map/jit(_take)/gather | solution.py:116
  296.1 10.3 %bitcast_add_fusion.1 = f32[96,32,128]{2,1,0:T(8,128)} fusion(f32[12,8,32,128]{3,2,1,0:T(8,128)} %get-tuple-element.37, bf16[96,64,128]{2,1,0:T(8,128)(2,1)S(1)} %copy-done, f32[32,96,64]{2,0,1:T(8,128)S(1)} %copy-done.1, bf16[96,6,64,64]{3,2,1,0:T(8,128)(2,1)} %copy.71, bf16[96,6,64,32]{3,2,1,0:T(8,128)(2,1)} %gather.23, pred[96,6]{1,0:T(8,128)(4,1)S(1)} %copy-done.6, ...), kind=kOutput, calls=%fused_computation.44 | convolution fusion | flops 204472320 | bytes 12584640 | tf_op jit(solution)/shard_map/lkr,lkm->lrm/dot_general | solution.py:127
  (169 shorter events, 51.8 us)
Async XLA Ops:
  0.0 296.1 %copy-start = (bf16[96,64,128]{2,1,0:T(8,128)(2,1)S(1)}, bf16[96,64,128]{2,1,0:T(8,128)(2,1)}, u32[]{:S(2)}) copy-start(bf16[96,64,128]{2,1,0:T(8,128)(2,1)} %param.25) | copy-start | bytes 4718596
  4.9 274.1 %collective-permute-start.1 = (bf16[96,2048]{1,0:T(8,128)(2,1)}, bf16[96,2048]{1,0:T(8,128)(2,1)}, u32[]{:S(2)}, u32[]{:S(2)}) collective-permute-start(bf16[96,2048]{1,0:T(8,128)(2,1)} %copy.66), channel_id=1, source_target_pairs={{1,0},{2,1},{3,2},{4,3},{5,4},{6,5},{7,6},{8,7},{9,8},{10,9},{11,1... | collective-permute-start | bytes 1179656 | tf_op jit(solution)/shard_map/ppermute | solution.py:23
  14.2 264.8 %collective-permute-start = (bf16[96,2048]{1,0:T(8,128)(2,1)}, bf16[96,2048]{1,0:T(8,128)(2,1)}, u32[]{:S(2)}, u32[]{:S(2)}) collective-permute-start(bf16[96,2048]{1,0:T(8,128)(2,1)} %copy.66), channel_id=1, source_target_pairs={{0,1},{1,2},{2,3},{3,4},{4,5},{5,6},{6,7},{7,8},{8,9},{9,10},{10,1... | collective-permute-start | bytes 1179656 | tf_op jit(solution)/shard_map/ppermute | solution.py:21
  17.4 55.6 %collective-permute-start.9 = (f32[4,7,128]{2,1,0:T(8,128)S(1)}, f32[4,7,128]{2,1,0:T(8,128)S(1)}, u32[]{:S(2)}, u32[]{:S(2)}) collective-permute-start(f32[4,7,128]{2,1,0:T(8,128)S(1)} %get-tuple-element.82), channel_id=1, source_target_pairs={{0,1},{1,2},{2,3},{3,4},{4,5},{5,6},{6,7},{7,8},{8,9},{9,10},{10,1... | collective-permute-start | bytes 43016 | tf_op jit(solution)/shard_map/ppermute | solution.py:21
  19.3 14.0 %copy-start.5 = (bf16[1,64,64]{2,1,0:T(8,128)(2,1)S(1)}, bf16[1,64,64]{2,1,0:T(8,128)(2,1)}, u32[]{:S(2)}) copy-start(bf16[1,64,64]{2,1,0:T(8,128)(2,1)} %param.31) | copy-start | bytes 24580
  19.3 14.4 %copy-start.10 = (s32[1,6]{1,0:T(1,128)S(1)}, s32[1,6]{1,0:T(1,128)}, u32[]{:S(2)}) copy-start(s32[1,6]{1,0:T(1,128)} %param.34) | copy-start | bytes 76
  19.3 14.5 %copy-start.11 = (s32[1,6]{1,0:T(1,128)S(1)}, s32[1,6]{1,0:T(1,128)}, u32[]{:S(2)}) copy-start(s32[1,6]{1,0:T(1,128)} %param.38) | copy-start | bytes 76
  19.3 15.8 %copy-start.9 = (s32[96]{0:T(128)S(1)}, s32[96]{0:T(128)}, u32[]{:S(2)}) copy-start(s32[96]{0:T(128)} %param.30) | copy-start | bytes 1156
  19.3 16.5 %copy-start.7 = (s32[96,6]{0,1:T(8,128)S(1)}, s32[96,6]{0,1:T(8,128)}, u32[]{:S(2)}) copy-start(s32[96,6]{0,1:T(8,128)} %param.29) | copy-start | bytes 6916
  19.3 16.7 %copy-start.8 = (s32[96,8]{0,1:T(8,128)S(1)}, s32[96,8]{0,1:T(8,128)}, u32[]{:S(2)}) copy-start(s32[96,8]{0,1:T(8,128)} %param.23) | copy-start | bytes 9220
  19.4 57.3 %collective-permute-start.10 = (f32[4,7,128]{2,1,0:T(8,128)S(1)}, f32[4,7,128]{2,1,0:T(8,128)S(1)}, u32[]{:S(2)}, u32[]{:S(2)}) collective-permute-start(f32[4,7,128]{2,1,0:T(8,128)S(1)} %get-tuple-element.83), channel_id=1, source_target_pairs={{1,0},{2,1},{3,2},{4,3},{5,4},{6,5},{7,6},{8,7},{9,8},{10,9},{11,1... | collective-permute-start | bytes 43016 | tf_op jit(solution)/shard_map/ppermute | solution.py:23
  33.6 4.1 %collective-permute-start.4 = (f32[1,2048]{1,0:T(1,128)S(1)}, f32[1,2048]{1,0:T(1,128)S(1)}, u32[]{:S(2)}, u32[]{:S(2)}) collective-permute-start(f32[1,2048]{1,0:T(1,128)S(1)} %reshape.189), channel_id=1, source_target_pairs={{0,1},{1,0},{2,3},{3,2},{4,5},{5,4},{6,7},{7,6},{8,9},{9,8},{10,11... | collective-permute-start | bytes 24584 | tf_op jit(solution)/shard_map/ppermute | solution.py:89
  37.8 33.0 %collective-permute-start.5 = (f32[1,2048]{1,0:T(1,128)S(1)}, f32[1,2048]{1,0:T(1,128)S(1)}, u32[]{:S(2)}, u32[]{:S(2)}) collective-permute-start(f32[1,2048]{1,0:T(1,128)S(1)} %add.124), channel_id=1, source_target_pairs={{0,2},{1,3},{2,0},{3,1},{4,6},{5,7},{6,4},{7,5},{8,10},{9,11},{10,... | collective-permute-start | bytes 24584 | tf_op jit(solution)/shard_map/ppermute | solution.py:89
  54.7 78.8 %copy-start.2 = (bf16[32,64,64]{2,1,0:T(8,128)(2,1)S(1)}, bf16[32,64,64]{2,1,0:T(8,128)(2,1)}, u32[]{:S(2)}) copy-start(bf16[32,64,64]{2,1,0:T(8,128)(2,1)} %param.35) | copy-start | bytes 786436
  70.8 66.7 %collective-permute-start.3 = (bf16[8,2048]{1,0:T(8,128)(2,1)S(1)}, bf16[8,2048]{1,0:T(8,128)(2,1)S(1)}, u32[]{:S(2)}, u32[]{:S(2)}) collective-permute-start(bf16[8,2048]{1,0:T(8,128)(2,1)S(1)} %bitcast.164), channel_id=1, source_target_pairs={{8,0},{16,8},{24,16},{32,24},{40,32},{48,40},{56,48},{64,56},{72,6... | collective-permute-start | bytes 98312 | tf_op jit(solution)/shard_map/ppermute | solution.py:23
  72.9 66.6 %collective-permute-start.2 = (bf16[8,2048]{1,0:T(8,128)(2,1)S(1)}, bf16[8,2048]{1,0:T(8,128)(2,1)S(1)}, u32[]{:S(2)}, u32[]{:S(2)}) collective-permute-start(bf16[8,2048]{1,0:T(8,128)(2,1)S(1)} %bitcast.165), channel_id=1, source_target_pairs={{0,8},{8,16},{16,24},{24,32},{32,40},{40,48},{48,56},{56,64},{64,7... | collective-permute-start | bytes 98312 | tf_op jit(solution)/shard_map/ppermute | solution.py:21
  76.7 5.2 %collective-permute-start.6 = (f32[1,2048]{1,0:T(1,128)S(1)}, f32[1,2048]{1,0:T(1,128)S(1)}, u32[]{:S(2)}, u32[]{:S(2)}) collective-permute-start(f32[1,2048]{1,0:T(1,128)S(1)} %add.125), channel_id=1, source_target_pairs={{0,4},{1,5},{2,6},{3,7},{4,0},{5,1},{6,2},{7,3},{8,12},{9,13},{10,... | collective-permute-start | bytes 24584 | tf_op jit(solution)/shard_map/ppermute | solution.py:89
  81.9 59.0 %collective-permute-start.7 = (bf16[4,32,128]{2,1,0:T(8,128)(2,1)S(1)}, bf16[4,32,128]{2,1,0:T(8,128)(2,1)S(1)}, u32[]{:S(2)}, u32[]{:S(2)}) collective-permute-start(bf16[4,32,128]{2,1,0:T(8,128)(2,1)S(1)} %get-tuple-element.80), channel_id=1, source_target_pairs={{0,1},{1,2},{2,3},{3,4},{4,5},{5,6},{6,7},{7,8},{8,9},{9,10},{10,1... | collective-permute-start | bytes 98312 | tf_op jit(solution)/shard_map/ppermute | solution.py:21
  137.5 4.1 %collective-permute-start.8 = (bf16[4,32,128]{2,1,0:T(8,128)(2,1)S(1)}, bf16[4,32,128]{2,1,0:T(8,128)(2,1)S(1)}, u32[]{:S(2)}, u32[]{:S(2)}) collective-permute-start(bf16[4,32,128]{2,1,0:T(8,128)(2,1)S(1)} %get-tuple-element.81), channel_id=1, source_target_pairs={{1,0},{2,1},{3,2},{4,3},{5,4},{6,5},{7,6},{8,7},{9,8},{10,9},{11,1... | collective-permute-start | bytes 98312 | tf_op jit(solution)/shard_map/ppermute | solution.py:23
  141.0 0.6 copy-start.3
  284.4 11.7 %copy-start.1 = (f32[32,96,64]{2,0,1:T(8,128)S(1)}, f32[32,96,64]{2,0,1:T(8,128)}, u32[]{:S(2)}) copy-start(f32[32,96,64]{2,0,1:T(8,128)} %fusion.37) | copy-start | bytes 2359300
  284.4 11.7 %copy-start.4 = (bf16[96,6]{1,0:T(8,128)(2,1)S(1)}, bf16[96,6]{1,0:T(8,128)(2,1)}, u32[]{:S(2)}) copy-start(bf16[96,6]{1,0:T(8,128)(2,1)} %fusion.49) | copy-start | bytes 3460
  284.4 11.7 %copy-start.6 = (pred[96,6]{1,0:T(8,128)(4,1)S(1)}, pred[96,6]{1,0:T(8,128)(4,1)}, u32[]{:S(2)}) copy-start(pred[96,6]{1,0:T(8,128)(4,1)} %copy.64) | copy-start | bytes 1732
